TPU v7x, 128 devices: a whole 4x4x4 slice. The times are simulated.
128 devices in a mesh: ctx: 64 (over z, y, x), head: 2 (over core).
Axes of the slice: x: 4, y: 4, z: 4, core: 2. Of those that a mesh axis runs over, the one named last changes fastest.
Arguments:
- query: bfloat16 [24576, 6144], P(('ctx', 'head')), may hold values from -6 to 6
- key_in: bfloat16 [24576, 6144], P(('ctx', 'head')), may hold values from -6 to 6
- value: bfloat16 [24576, 6144], P(('ctx', 'head')), may hold values from -6 to 6
- cotangent: bfloat16 [24576, 6144], P(('ctx', 'head')), may hold values from -18 to 18
- decay_rate: float32 [48, 16], replicated, as said below
- residue: float32 [48, 16], replicated, may hold values from -2 to 2
Outputs:
- mixed: bfloat16 [24576, 6144], P(('ctx', 'head'))
- grad_query: bfloat16 [24576, 6144], P(('ctx', 'head'))
- grad_key: bfloat16 [24576, 6144], P(('ctx', 'head'))
- grad_value: bfloat16 [24576, 6144], P(('ctx', 'head'))
- residue_grad: float32 [48, 16], P('head')
Inputs may be any that keep to these rules, and one draw needn't show every extreme that they name: `decay_rate`: positive decay rates of at most 1/30.
All inputs are finite; a program needn't handle non-finite values.
Results may differ from a plain program's by a relative error of at most 0.00105.
Values may be sent and summed in bfloat16 or wider, within the bound.
No kernel may reach another device: no remote copies, remote signals or barrier semaphores. Data moves between devices by JAX's collectives and lax.ppermute only.
A program may use at most 192 MiB of HBM per device.

v0:
```python
import math
import jax
import jax.numpy as jnp
from jax import lax
from jax.sharding import PartitionSpec as P

HEAD_DIM = 128
SPAN = 768
HIGHEST = lax.Precision.HIGHEST


def entering_2(part, axis, combine, identity, reverse):
    count = lax.axis_size(axis)
    place = lax.axis_index(axis)
    ahead = count - 1 - place if reverse else place
    gathered = jax.tree.map(lambda a: lax.all_gather(a, axis), part)
    state = jax.tree.map(lambda a, e: jnp.zeros_like(a) + jnp.asarray(e, a.dtype), part, identity)

    def one(lap, state):
        source = count - 1 - lap if reverse else lap
        return combine(
            state, jax.tree.map(lambda a: lax.dynamic_index_in_dim(a, source, 0, False), gathered)
        )

    return lax.fori_loop(0, ahead, one, state)


def combine_states(earlier, later_part):
    return (earlier[0] * later_part[0], later_part[0][..., None] * earlier[1] + later_part[1])


def modal_layer(
    query,
    key_in,
    value,
    cotangent,
    decay_rate,
    residue,
    block_rows,
    forward_chain,
    backward_chain,
    seq_total,
):
    row_count, feature_count = query.shape
    head_count = decay_rate.shape[0]
    head_size = feature_count // head_count
    block_count = row_count // block_rows

    def blocked(source):
        return source.reshape(block_count, block_rows, head_count, head_size).astype(jnp.float32)

    query_wide = blocked(query)
    key_wide = blocked(key_in)
    value_wide = blocked(value)
    cotan_wide = blocked(cotangent)
    product = key_wide * value_wide
    norm_factor = jnp.sqrt(-jnp.expm1(-2.0 * decay_rate))
    coefficient = residue * norm_factor
    offsets = jnp.arange(block_rows, dtype=jnp.float32)
    decay_in = jnp.exp(-decay_rate[:, :, None] * offsets)
    decay_end = jnp.exp(-decay_rate[:, :, None] * (float(block_rows - 1) - offsets))
    growth = jnp.exp(decay_rate[:, :, None] * offsets)
    one_step = jnp.exp(-decay_rate)
    lag_index = lax.broadcasted_iota(jnp.int32, (block_rows, block_rows), 0) - lax.broadcasted_iota(
        jnp.int32, (block_rows, block_rows), 1
    )
    lower = lag_index[None] >= 0
    weighted_in = coefficient[:, :, None] * decay_in
    full_table = jnp.einsum("hmi,hmj->hij", weighted_in, growth, precision=HIGHEST)
    toeplitz = jnp.where(lower, full_table, 0.0)
    inner_part = jnp.einsum("hij,bjhc->bihc", toeplitz, product, precision=HIGHEST)
    block_ends = jnp.einsum("hmj,bjhc->bhmc", decay_end, product, precision=HIGHEST)
    block_decay = jnp.exp(-decay_rate * block_rows)[:, :, None]

    def walk_forward(state, block_end):
        return (block_decay * state + block_end, state)

    zero_state = jnp.zeros(block_ends.shape[1:], jnp.float32)
    device_total, entering_local = lax.scan(walk_forward, zero_state, block_ends)
    device_decay = jnp.exp(-decay_rate * row_count)
    incoming = forward_chain(device_decay, device_total)
    block_starts = jnp.arange(block_count, dtype=jnp.float32) * block_rows
    block_powers = jnp.exp(-decay_rate[None] * block_starts[:, None, None])[..., None]
    later_starts = (
        float(block_count - 1) - jnp.arange(block_count, dtype=jnp.float32)
    ) * block_rows
    later_powers = jnp.exp(-decay_rate[None] * later_starts[:, None, None])[..., None]
    entering = entering_local + block_powers * incoming[None]
    inflow = coefficient[:, :, None] * one_step[:, :, None] * decay_in
    outer_part = jnp.einsum("hmi,bhmc->bihc", inflow, entering, precision=HIGHEST)
    convolved = inner_part + outer_part
    mixed = (query_wide * convolved).reshape(row_count, feature_count).astype(jnp.bfloat16)
    grad_conv = cotan_wide * query_wide
    grad_query = (cotan_wide * convolved).reshape(row_count, feature_count).astype(jnp.bfloat16)
    back_inner = jnp.einsum("hij,bihc->bjhc", toeplitz, grad_conv, precision=HIGHEST)
    block_heads = jnp.einsum("hmi,bihc->bhmc", decay_in, grad_conv, precision=HIGHEST)

    def walk_backward(state, block_head):
        return (block_decay * state + block_head, state)

    back_total, later_local = lax.scan(walk_backward, zero_state, block_heads, reverse=True)
    outgoing = backward_chain(device_decay, back_total)
    later_states = later_local + later_powers * outgoing[None]
    outflow = coefficient[:, :, None] * one_step[:, :, None] * decay_end
    back_outer = jnp.einsum("hmj,bhmc->bjhc", outflow, later_states, precision=HIGHEST)
    grad_product = back_inner + back_outer
    grad_key = (grad_product * value_wide).reshape(row_count, feature_count).astype(jnp.bfloat16)
    grad_value = (grad_product * key_wide).reshape(row_count, feature_count).astype(jnp.bfloat16)
    cross_table = jnp.einsum("bihc,bjhc->hij", grad_conv, product, precision=HIGHEST)
    cross_lower = jnp.where(lower, cross_table, 0.0)
    grown_rows = jnp.einsum("hij,hmj->hmi", cross_lower, growth, precision=HIGHEST)
    near_terms = jnp.sum(grown_rows * decay_in, axis=2)
    far_terms = one_step * jnp.einsum("bhmc,bhmc->hm", block_heads, entering, precision=HIGHEST)
    residue_terms = norm_factor * (near_terms + far_terms) / math.sqrt(float(seq_total * HEAD_DIM))
    return (mixed, grad_query, grad_key, grad_value, residue_terms)


def on_device(query, key_in, value, cotangent, decay_rate, residue):
    seq_total = query.shape[0] * lax.axis_size("ctx") * lax.axis_size("head")
    group_heads = decay_rate.shape[0] // lax.axis_size("head")
    first_head = lax.axis_index("head") * group_heads
    local_rates = lax.dynamic_slice_in_dim(decay_rate, first_head, group_heads, 0)
    local_residue = lax.dynamic_slice_in_dim(residue, first_head, group_heads, 0)
    arrived = (
        lax.all_to_all(query, "head", split_axis=1, concat_axis=0, tiled=True),
        lax.all_to_all(key_in, "head", split_axis=1, concat_axis=0, tiled=True),
        lax.all_to_all(value, "head", split_axis=1, concat_axis=0, tiled=True),
        lax.all_to_all(cotangent, "head", split_axis=1, concat_axis=0, tiled=True),
    )
    block_rows = min(SPAN, arrived[0].shape[0])

    def forward_chain(decays, totals):
        return entering_2(
            (decays, totals),
            "ctx",
            combine_states,
            (jnp.ones_like(decays), jnp.zeros_like(totals)),
            False,
        )[1]

    def backward_chain(decays, totals):
        return entering_2(
            (decays, totals),
            "ctx",
            combine_states,
            (jnp.ones_like(decays), jnp.zeros_like(totals)),
            True,
        )[1]

    results = modal_layer(
        arrived[0],
        arrived[1],
        arrived[2],
        arrived[3],
        local_rates,
        local_residue,
        block_rows,
        forward_chain,
        backward_chain,
        seq_total,
    )
    returned = (
        lax.all_to_all(results[0], "head", split_axis=0, concat_axis=1, tiled=True),
        lax.all_to_all(results[1], "head", split_axis=0, concat_axis=1, tiled=True),
        lax.all_to_all(results[2], "head", split_axis=0, concat_axis=1, tiled=True),
        lax.all_to_all(results[3], "head", split_axis=0, concat_axis=1, tiled=True),
    )
    residue_grad = lax.psum(results[4], "ctx")
    return (returned[0], returned[1], returned[2], returned[3], residue_grad)


def solution(mesh):
    placed = (
        P(("ctx", "head"), None),
        P(("ctx", "head"), None),
        P(("ctx", "head"), None),
        P(("ctx", "head"), None),
        P(),
        P(),
    )
    return jax.shard_map(
        on_device,
        mesh=mesh,
        in_specs=placed,
        out_specs=(
            P(("ctx", "head"), None),
            P(("ctx", "head"), None),
            P(("ctx", "head"), None),
            P(("ctx", "head"), None),
            P("head", None),
        ),
        check_vma=False,
    )
```

profile of v0, /device:TPU:1, one launch (start us, length us, event | category | flops | bytes accessed | tf_op | source)
XLA Modules:
  0.0 1042.2 jit_solution(16150171669965274029)
XLA Ops:
  7.2 3.3 copy.159
  10.4 5.2 all-to-all-start.2
  15.8 3.2 copy.160
  19.1 6.6 all_to_all.116
  30.1 4.2 fusion.37
  34.3 3.2 copy.158
  37.6 5.3 all-to-all-start.4
  42.8 3.2 copy.161
  46.1 6.6 all_to_all.117
  52.7 3.4 convert_multiply_fusion
  59.2 155.4 %all-gather.1 = f32[64,24,16]{1,2,0:T(8,128)S(1)} all-gather(f32[1,24,16]{1,2,0:T(8,128)S(1)} %copy.92), channel_id=2, replica_groups=mesh['ctx'=64,'head'=2] {'ctx'}, dimensions={0}, use_global_device_ids=true | all-gather | bytes 99840 | tf_op jit(solution)/shard_map/all_gather | solution.py:16
  215.9 11.2 %while.16 = (s32[]{:T(128)}, f32[24,16,128]{2,1,0:T(8,128)S(1)}, s32[]{:T(128)}, f32[64,24,16]{2,1,0:T(8,128)}, f32[64,24,16,128]{3,2,1,0:T(8,128)}, /*index=5*/s32[]{:T(128)}, s32[]{:T(128)}, s32[]{:T(128)}) while((s32[]{:T(128)}, f32[24,16,128]{2,1,0:T(8,128)S(1)}, s32[]{:T(128)}, f32[64,24,16]{2,1,0:T(8,128)}, ...), condition=%wide.region_1.2_spmd, body=%wide.region_0.1_spmd.sunk | while | flops 98309 | bytes 594567 | solution.py:25
  227.1 5.9 fusion.56
  236.0 3.2 copy.130
  239.2 6.1 copy.99
  247.5 3.2 copy.128
  250.7 6.1 copy.95
  262.2 6.0 copy.108
  271.9 6.1 copy.105
  278.0 15.8 %fusion.17 = f32[24,384,384]{2,1,0:T(8,128)S(1)} fusion(f32[384,24,128]{2,1,0:T(8,128)} %bitcast.123, f32[384,24,128]{2,1,0:T(8,128)} %bitcast.118), kind=kOutput, calls=%fused_computation.25 | convolution fusion | flops 5435817984 | bytes 23592960 | tf_op jit(solution)/shard_map/bihc,bjhc->hij/dot_general | solution.py:109
  293.9 13.5 %fusion.28 = f32[24,16]{1,0:T(8,128)S(1)} fusion(f32[24,384,384]{2,1,0:T(8,128)S(1)} %fusion.17, pred[384,384]{1,0:T(8,128)(4,1)S(1)} %subtract_compare_fusion, f32[24,16]{1,0:T(8,128)S(1)} %copy.119, f32[24,16]{1,0:T(8,128)S(1)} %get-tuple-element.240), kind=kOutput, calls=%fused_computation.42 | convolution fusion | flops 683605632 | bytes 14307840 | tf_op jit(solution)/shard_map/hij,hmj->hmi/dot_general | solution.py:111
  307.4 14.3 %fusion.42 = f32[24,384,384]{2,1,0:T(8,128)} fusion(f32[24,16]{1,0:T(8,128)S(1)} %copy.119, f32[24,16]{1,0:T(8,128)S(1)} %get-tuple-element.240, f32[24,16]{1,0:T(8,128)S(1)} %get-tuple-element.231), kind=kOutput, calls=%fused_computation.50 | convolution fusion | flops 679919616 | bytes 14160384 | tf_op jit(solution)/shard_map/hmi,hmj->hij/dot_general | solution.py:69
  321.8 23.5 %fusion.4 = f32[24,128,384]{2,1,0:T(8,128)} fusion(f32[24,384,384]{2,1,0:T(8,128)} %fusion.42, pred[384,384]{1,0:T(8,128)(4,1)S(1)} %subtract_compare_fusion, f32[384,24,128]{2,1,0:T(8,128)S(1)} %bitcast.121), kind=kOutput, calls=%fused_computation.8 | convolution fusion | flops 5439356928 | bytes 23740416 | tf_op jit(solution)/shard_map/hij,bjhc->bihc/dot_general | solution.py:71
  345.3 9.6 fusion.15
  360.4 34.3 %all_to_all.118 = bf16[2,192,3072]{2,1,0:T(8,128)(2,1)S(1)} all-to-all(bf16[2,192,3072]{2,1,0:T(8,128)(2,1)} %convert_element_type.134), channel_id=1, replica_groups=mesh['ctx'=64,'head'=2] {'head'}, dimensions={0} | all-to-all | bytes 4718592 | tf_op jit(solution)/shard_map/all_to_all | solution.py:163
  401.8 6.9 all_to_all.119
  410.3 398.9 %psum.7 = f32[24,16]{1,0:T(8,128)S(1)} all-reduce(f32[24,16]{1,0:T(8,128)S(1)} %get-tuple-element.236), channel_id=1, replica_groups=mesh['ctx'=64,'head'=2] {'ctx'}, use_global_device_ids=true, to_apply=%region_5.6 | all-reduce | flops 384 | bytes 3072 | tf_op jit(solution)/shard_map/psum | solution.py:168
  809.9 19.5 %fusion.2 = f32[24,128,384]{2,1,0:T(8,128)} fusion(f32[24,384,384]{2,1,0:T(8,128)} %fusion.42, pred[384,384]{1,0:T(8,128)(4,1)S(1)} %subtract_compare_fusion, f32[384,24,128]{2,1,0:T(8,128)} %bitcast.124), kind=kOutput, calls=%fused_computation.6 | convolution fusion | flops 5439356928 | bytes 23740416 | tf_op jit(solution)/shard_map/hij,bihc->bjhc/dot_general | solution.py:95
  829.5 112.8 %while.17 = (s32[]{:T(128)}, f32[24,16,128]{2,1,0:T(8,128)S(1)}, s32[]{:T(128)}, f32[64,24,16]{2,1,0:T(8,128)}, f32[64,24,16,128]{3,2,1,0:T(8,128)}, /*index=5*/s32[]{:T(128)}, s32[]{:T(128)}, s32[]{:T(128)}, s32[]{:T(128)}) while((s32[]{:T(128)}, f32[24,16,128]{2,1,0:T(8,128)S(1)}, s32[]{:T(128)}, f32[64,24,16]{2,1,0:T(8,128)}, ...), condition=%wide.region_3.4_spmd, body=%wide.region_2.3_spmd.sunk | while | flops 98310 | bytes 594587 | solution.py:25
  942.3 9.6 fusion.13
  957.4 62.1 %all_to_all.120 = bf16[2,192,3072]{2,1,0:T(8,128)(2,1)S(1)} all-to-all(bf16[2,192,3072]{2,1,0:T(8,128)(2,1)} %convert_element_type.146), channel_id=1, replica_groups=mesh['ctx'=64,'head'=2] {'head'}, dimensions={0} | all-to-all | bytes 4718592 | tf_op jit(solution)/shard_map/all_to_all | solution.py:165
  1026.6 6.8 all_to_all.121
  (183 shorter events, 163.7 us)
Async XLA Ops:
  7.2 8.5 copy-start.3
  7.2 8.5 copy-start.4
  10.4 8.6 all-to-all-start.2
  15.6 200.3 %all-gather.5.cloned.1.call-start = ((), (), s32[]{:S(2)}) async-start(), calls=%async_computation.8 | async-start | bytes 12779520 | tf_op jit(solution)/shard_map/all_gather | solution.py:16
  25.6 1.4 copy-start.1
  28.0 2.1 copy-start
  37.6 8.5 all-to-all-start.4
  42.8 786.6 %all-gather.7.cloned.1.call-start = ((), (), s32[]{:S(2)}) async-start(), calls=%async_computation.9 | async-start | bytes 12779520 | tf_op jit(solution)/shard_map/all_gather | solution.py:16
  52.7 3.4 copy-start.2
  293.9 27.9 %slice-start = ((s8[4718592]{0:T(1024)(128)(4,1)}), s8[4194304]{0:T(1024)(128)(4,1)S(1)}, s32[]{:S(2)}) async-start(s8[4718592]{0:T(1024)(128)(4,1)} %bitcast.119), calls=%async_computation.10 | async-start | bytes 8388608
  307.4 14.4 %slice-start.1 = ((s8[4718592]{0:T(1024)(128)(4,1)}), s8[524288]{0:T(1024)(128)(4,1)S(1)}, s32[]{:S(2)}) async-start(s8[4718592]{0:T(1024)(128)(4,1)} %bitcast.119), calls=%async_computation.11 | async-start | bytes 1048576
Sparse Core Ops, SparseCore 0:
  34.5 94.2 all-gather.4
  233.9 224.1 all-gather.6
where the time goes:
time: 1050 us; the launch traced here: 1040 us
  blocking collectives  678 us (65%)
  local copies, waits for them, and re-layouts  132 us (13%)
  matrix products  116 us (11%)
  other arithmetic  78.4 us (7%)
  between operations  14.5 us (1%)
  loops' own time  13 us (1%)
    psum x1, blocking collectives, on_device(): residue_grad = lax.psum(results[4], 'ctx')  399 us
    all_gather x1, blocking collectives, entering_2(): gathered = jax.tree.map(lambda a: lax.all_gather(a, axis), part)  155 us
    add x63, other arithmetic, combine_states(): later_part[0][..., None] * earlier[1] + later_part[1]  66.1 us
    all_to_all x1, blocking collectives, on_device(): lax.all_to_all(results[2], 'head', split_axis=0, concat_axis=1, tiled=True)  62.1 us
    mul x63, local copies, waits for them, and re-layouts, combine_states(): later_part[0][..., None] * earlier[1] + later_part[1]  44.9 us
    all_to_all x1, blocking collectives, on_device(): lax.all_to_all(results[0], 'head', split_axis=0, concat_axis=1, tiled=True)  34.3 us
    convert_element_type x4, local copies, waits for them, and re-layouts, blocked(): source.reshape(block_count, block_rows, head_count, head_size)  24.3 us
    dot_general x1, matrix products, modal_layer(): jnp.einsum('hij,bjhc->bihc', toeplitz, product, precision=HIGHEST)  23.5 us
  transfers between devices with their start and end apart: 4, of which 0 were waited for; matrix products, arithmetic and copies ran while one was open for 17% of the time, Pallas kernels for 0%

commit v1 on v0

--- a/solution.py
+++ b/solution.py
@@ -165,7 +165,7 @@
         lax.all_to_all(results[2], "head", split_axis=0, concat_axis=1, tiled=True),
         lax.all_to_all(results[3], "head", split_axis=0, concat_axis=1, tiled=True),
     )
-    residue_grad = lax.psum(results[4], "ctx")
+    residue_grad = jnp.sum(lax.all_gather(results[4], "ctx"), axis=0)
     return (returned[0], returned[1], returned[2], returned[3], residue_grad)
 
 

time: 1050 us -> 886 us (0.84)
  blocking collectives: 678 us -> 508 us
    psum x1 -> x0, blocking collectives: 399 us -> none  [on_device(): residue_grad = lax.psum(results[4], 'ctx')]
    all_gather x0 -> x1, blocking collectives: none -> 257 us  [on_device(): residue_grad = jnp.sum(lax.all_gather(results[4], 'ctx'), axis=0)]
    all_to_all x1, blocking collectives: 62.1 us -> 35 us  [on_device(): lax.all_to_all(results[2], 'head', split_axis=0, concat_axis=1, tiled=True)]
  transfers between devices with their start and end apart: 4 -> 4, of which waited for: 0 -> 0; matrix products, arithmetic and copies ran while one was open for 17% -> 20% of each run, Pallas kernels for 0% -> 0%
where the time goes in v1:
time: 886 us; the launch traced here: 873 us
  blocking collectives  508 us (57%)
  local copies, waits for them, and re-layouts  132 us (15%)
  matrix products  116 us (13%)
  other arithmetic  79.1 us (9%)
  between operations  14.5 us (2%)
  loops' own time  13 us (1%)
  starting transfers between devices  10.4 us (1%)
    all_gather x1, blocking collectives, on_device(): residue_grad = jnp.sum(lax.all_gather(results[4], 'ctx'), axis=0)  257 us
    all_gather x1, blocking collectives, entering_2(): gathered = jax.tree.map(lambda a: lax.all_gather(a, axis), part)  155 us
    add x63, other arithmetic, combine_states(): later_part[0][..., None] * earlier[1] + later_part[1]  66.1 us
    mul x63, local copies, waits for them, and re-layouts, combine_states(): later_part[0][..., None] * earlier[1] + later_part[1]  44.9 us
    all_to_all x1, blocking collectives, on_device(): lax.all_to_all(results[2], 'head', split_axis=0, concat_axis=1, tiled=True)  35 us
    all_to_all x1, blocking collectives, on_device(): lax.all_to_all(results[0], 'head', split_axis=0, concat_axis=1, tiled=True)  34.3 us
    convert_element_type x4, local copies, waits for them, and re-layouts, blocked(): source.reshape(block_count, block_rows, head_count, head_size)  24.3 us
    dot_general x1, matrix products, modal_layer(): jnp.einsum('hij,bjhc->bihc', toeplitz, product, precision=HIGHEST)  23.5 us
  transfers between devices with their start and end apart: 4, of which 0 were waited for; matrix products, arithmetic and copies ran while one was open for 20% of the time, Pallas kernels for 0%

profile of v1, /device:TPU:1, one launch (start us, length us, event | category | flops | bytes accessed | tf_op | source)
XLA Modules:
  0.0 872.7 jit_solution(5716490613937317399)
XLA Ops:
  7.2 3.3 copy.174
  10.4 5.2 all-to-all-start.2
  15.8 3.2 copy.175
  19.1 6.6 all_to_all.116
  30.1 4.2 fusion.37
  34.3 3.2 copy.173
  37.6 5.3 all-to-all-start.4
  42.8 3.2 copy.176
  46.1 6.6 all_to_all.117
  52.7 3.4 convert_multiply_fusion
  59.2 155.4 %all-gather.2 = f32[64,24,16]{1,2,0:T(8,128)S(1)} all-gather(f32[1,24,16]{1,2,0:T(8,128)S(1)} %copy.104), channel_id=2, replica_groups=mesh['ctx'=64,'head'=2] {'ctx'}, dimensions={0}, use_global_device_ids=true | all-gather | bytes 99840 | tf_op jit(solution)/shard_map/all_gather | solution.py:16
  215.9 11.2 %while.16 = (s32[]{:T(128)}, f32[24,16,128]{2,1,0:T(8,128)S(1)}, s32[]{:T(128)}, f32[64,24,16]{2,1,0:T(8,128)}, f32[64,24,16,128]{3,2,1,0:T(8,128)}, /*index=5*/s32[]{:T(128)}, s32[]{:T(128)}, s32[]{:T(128)}) while((s32[]{:T(128)}, f32[24,16,128]{2,1,0:T(8,128)S(1)}, s32[]{:T(128)}, f32[64,24,16]{2,1,0:T(8,128)}, ...), condition=%wide.region_1.2_spmd, body=%wide.region_0.1_spmd.sunk | while | flops 98309 | bytes 594567 | solution.py:25
  227.1 5.9 fusion.56
  236.0 3.2 copy.145
  239.2 6.1 copy.111
  247.5 3.2 copy.143
  250.7 6.1 copy.107
  262.2 6.0 copy.120
  271.9 6.1 copy.117
  278.0 15.8 %fusion.17 = f32[24,384,384]{2,1,0:T(8,128)S(1)} fusion(f32[384,24,128]{2,1,0:T(8,128)} %bitcast.120, f32[384,24,128]{2,1,0:T(8,128)} %bitcast.123), kind=kOutput, calls=%fused_computation.25 | convolution fusion | flops 5435817984 | bytes 23592960 | tf_op jit(solution)/shard_map/bihc,bjhc->hij/dot_general | solution.py:109
  293.9 13.5 %fusion.28 = f32[24,16]{1,0:T(8,128)S(1)} fusion(f32[24,384,384]{2,1,0:T(8,128)S(1)} %fusion.17, pred[384,384]{1,0:T(8,128)(4,1)S(1)} %subtract_compare_fusion, f32[24,16]{1,0:T(8,128)S(1)} %copy.133, f32[24,16]{1,0:T(8,128)S(1)} %get-tuple-element.225), kind=kOutput, calls=%fused_computation.42 | convolution fusion | flops 683605632 | bytes 14307840 | tf_op jit(solution)/shard_map/hij,hmj->hmi/dot_general | solution.py:111
  307.4 14.3 %fusion.42 = f32[24,384,384]{2,1,0:T(8,128)} fusion(f32[24,16]{1,0:T(8,128)S(1)} %copy.133, f32[24,16]{1,0:T(8,128)S(1)} %get-tuple-element.225, f32[24,16]{1,0:T(8,128)S(1)} %get-tuple-element.216), kind=kOutput, calls=%fused_computation.50 | convolution fusion | flops 679919616 | bytes 14160384 | tf_op jit(solution)/shard_map/hmi,hmj->hij/dot_general | solution.py:69
  321.8 23.5 %fusion.4 = f32[24,128,384]{2,1,0:T(8,128)} fusion(f32[24,384,384]{2,1,0:T(8,128)} %fusion.42, pred[384,384]{1,0:T(8,128)(4,1)S(1)} %subtract_compare_fusion, f32[384,24,128]{2,1,0:T(8,128)S(1)} %bitcast.126), kind=kOutput, calls=%fused_computation.8 | convolution fusion | flops 5439356928 | bytes 23740416 | tf_op jit(solution)/shard_map/hij,bjhc->bihc/dot_general | solution.py:71
  345.3 9.6 %fusion.15 = (bf16[1,384,24,128]{1,3,2,0:T(8,128)(2,1)}, bf16[1,384,24,128]{1,3,2,0:T(8,128)(2,1)}) fusion(f32[1,384,24,128]{1,3,2,0:T(8,128)} %copy.111, f32[1,384,24,128]{1,3,2,0:T(8,128)} %copy.107, f32[24,128,384]{2,1,0:T(8,128)} %fusion.4, f32[24,16]{1,0:T(8,128)S(1)} %get-tuple-element.215, f32[24,16]{1,0:T(8,128)S(1)} %get-tuple-element.225, ...), kind=kOutput, calls=%fused_computation.23 | convolution fusion | flops 232734720 | bytes 19075584 | tf_op jit(solution)/shard_map/hmi,bhmc->bihc/dot_general | solution.py:90
  360.4 34.3 %all_to_all.118 = bf16[2,192,3072]{2,1,0:T(8,128)(2,1)S(1)} all-to-all(bf16[2,192,3072]{2,1,0:T(8,128)(2,1)} %convert_element_type.134), channel_id=1, replica_groups=mesh['ctx'=64,'head'=2] {'head'}, dimensions={0} | all-to-all | bytes 4718592 | tf_op jit(solution)/shard_map/all_to_all | solution.py:163
  401.8 6.9 all_to_all.119
  410.4 256.6 %all-gather.3 = f32[64,24,16]{1,2,0:T(8,128)S(1)} all-gather(f32[1,24,16]{1,2,0:T(8,128)S(1)} %copy.125), channel_id=3, replica_groups=mesh['ctx'=64,'head'=2] {'ctx'}, dimensions={0}, use_global_device_ids=true | all-gather | bytes 99840 | tf_op jit(solution)/shard_map/all_gather | solution.py:168
  667.6 19.5 %fusion.2 = f32[24,128,384]{2,1,0:T(8,128)} fusion(f32[24,384,384]{2,1,0:T(8,128)} %fusion.42, pred[384,384]{1,0:T(8,128)(4,1)S(1)} %subtract_compare_fusion, f32[384,24,128]{2,1,0:T(8,128)} %bitcast.121), kind=kOutput, calls=%fused_computation.6 | convolution fusion | flops 5439356928 | bytes 23740416 | tf_op jit(solution)/shard_map/hij,bihc->bjhc/dot_general | solution.py:95
  687.2 112.8 %while.17 = (s32[]{:T(128)}, f32[24,16,128]{2,1,0:T(8,128)S(1)}, s32[]{:T(128)}, f32[64,24,16]{2,1,0:T(8,128)}, f32[64,24,16,128]{3,2,1,0:T(8,128)}, /*index=5*/s32[]{:T(128)}, s32[]{:T(128)}, s32[]{:T(128)}, s32[]{:T(128)}) while((s32[]{:T(128)}, f32[24,16,128]{2,1,0:T(8,128)S(1)}, s32[]{:T(128)}, f32[64,24,16]{2,1,0:T(8,128)}, ...), condition=%wide.region_3.4_spmd, body=%wide.region_2.3_spmd.sunk | while | flops 98310 | bytes 594587 | solution.py:25
  800.0 9.6 %fusion.13 = (bf16[1,384,24,128]{1,3,2,0:T(8,128)(2,1)}, bf16[1,384,24,128]{1,3,2,0:T(8,128)(2,1)}) fusion(f32[1,384,24,128]{1,3,2,0:T(8,128)} %copy.120, f32[1,384,24,128]{1,3,2,0:T(8,128)} %copy.117, f32[24,128,384]{2,1,0:T(8,128)} %fusion.2, f32[24,16]{1,0:T(8,128)S(1)} %get-tuple-element.215, f32[384]{0:T(512)S(1)} %iota_subtract_fusion, ...), kind=kOutput, calls=%fused_computation.19 | convolution fusion | flops 232734720 | bytes 19077120 | tf_op jit(solution)/shard_map/hmj,bhmc->bjhc/dot_general | solution.py:105
  815.1 35.0 %all_to_all.120 = bf16[2,192,3072]{2,1,0:T(8,128)(2,1)S(1)} all-to-all(bf16[2,192,3072]{2,1,0:T(8,128)(2,1)} %convert_element_type.146), channel_id=1, replica_groups=mesh['ctx'=64,'head'=2] {'head'}, dimensions={0} | all-to-all | bytes 4718592 | tf_op jit(solution)/shard_map/all_to_all | solution.py:165
  857.2 6.8 all_to_all.121
  (184 shorter events, 163.8 us)
Async XLA Ops:
  7.2 8.5 copy-start.3
  7.2 8.5 copy-start.4
  10.4 8.6 all-to-all-start.2
  15.6 200.3 %all-gather.7.cloned.1.call-start = ((), (), s32[]{:S(2)}) async-start(), calls=%async_computation.8 | async-start | bytes 12779520 | tf_op jit(solution)/shard_map/all_gather | solution.py:16
  25.6 1.4 copy-start.1
  28.0 2.1 copy-start
  37.6 8.5 all-to-all-start.4
  42.8 644.3 %all-gather.9.cloned.1.call-start = ((), (), s32[]{:S(2)}) async-start(), calls=%async_computation.9 | async-start | bytes 12779520 | tf_op jit(solution)/shard_map/all_gather | solution.py:16
  52.7 3.4 copy-start.2
  293.9 27.9 %slice-start = ((s8[4718592]{0:T(1024)(128)(4,1)}), s8[4194304]{0:T(1024)(128)(4,1)S(1)}, s32[]{:S(2)}) async-start(s8[4718592]{0:T(1024)(128)(4,1)} %bitcast.124), calls=%async_computation.10 | async-start | bytes 8388608
  307.4 14.4 %slice-start.1 = ((s8[4718592]{0:T(1024)(128)(4,1)}), s8[524288]{0:T(1024)(128)(4,1)S(1)}, s32[]{:S(2)}) async-start(s8[4718592]{0:T(1024)(128)(4,1)} %bitcast.124), calls=%async_computation.11 | async-start | bytes 1048576
Sparse Core Ops, SparseCore 0:
  34.5 94.2 all-gather.6
  233.9 224.8 all-gather.8
